TPU v7x, 32 devices: a whole 2x2x4 slice. The times are simulated.
32 devices in a mesh: dp: 4 (over y, core), row: 2 (over x), col: 4 (over z).
Axes of the slice: x: 2, y: 2, z: 4, core: 2. Of those that a mesh axis runs over, the one named last changes fastest.
Arguments:
- hidden_in: bfloat16 [5120, 2048], P(('dp', 'col'), 'row'), may hold values from -6 to 6
- seq_lengths: int32 [4], P('dp'), may hold values from 512 to 1280, as said below
- gain_attn: bfloat16 [2048], P('row'), may hold values from 0.5 to 1.5
- w_query: bfloat16 [2048, 2048], P('row', 'col'), may hold values from -0.125 to 0.125
- w_key: bfloat16 [2048, 2048], P('row', 'col'), may hold values from -0.125 to 0.125
- w_value: bfloat16 [2048, 2048], P('row', 'col'), may hold values from -0.125 to 0.125
- w_outgate: bfloat16 [2048, 2048], P('row', 'col'), may hold values from -0.125 to 0.125
- rank_down: bfloat16 [2048, 16], P('row'), may hold values from -0.125 to 0.125
- rank_up: bfloat16 [16, 2048], P(None, 'col'), may hold values from -1.5 to 1.5
- decay_bias: float32 [2048], P('col'), may hold values from -1 to 7
- gain_head: bfloat16 [512], P('row'), may hold values from 0.5 to 1.5
- w_output: bfloat16 [2048, 2048], P('col', 'row'), may hold values from -0.1875 to 0.1875
- gain_ffn: bfloat16 [2048], P('row'), may hold values from 0.5 to 1.5
- w_gate: bfloat16 [2048, 5632], P('row', 'col'), may hold values from -0.125 to 0.125
- w_up: bfloat16 [2048, 5632], P('row', 'col'), may hold values from -0.125 to 0.125
- w_down: bfloat16 [5632, 2048], P('col', 'row'), may hold values from -0.109375 to 0.109375
- cotangent: bfloat16 [5120, 2048], P(('dp', 'col'), 'row'), may hold values from -6 to 6
Outputs:
- block_out: bfloat16 [5120, 2048], P(('dp', 'col'), 'row')
- grad_input: float32 [5120, 2048], P(('dp', 'col'), 'row')
- grad_gain_attn: float32 [2048], P('row')
- grad_w_query: float32 [2048, 2048], P('row', 'col')
- grad_w_key: float32 [2048, 2048], P('row', 'col')
- grad_w_value: float32 [2048, 2048], P('row', 'col')
- grad_w_outgate: float32 [2048, 2048], P('row', 'col')
- grad_rank_down: float32 [2048, 16], P('row')
- grad_rank_up: float32 [16, 2048], P(None, 'col')
- grad_decay_bias: float32 [2048], P('col')
- grad_gain_head: float32 [512], P('row')
- grad_w_output: float32 [2048, 2048], P('col', 'row')
- grad_gain_ffn: float32 [2048], P('row')
- grad_w_gate: float32 [2048, 5632], P('row', 'col')
- grad_w_up: float32 [2048, 5632], P('row', 'col')
- grad_w_down: float32 [5632, 2048], P('col', 'row')
Inputs may be any that keep to these rules, and one draw needn't show every extreme that they name: `seq_lengths`: valid tokens of each slot of 1280 positions; every draw has one full slot and one slot of exactly 512 tokens.
All inputs are finite; a program needn't handle non-finite values.
Results may differ from a plain program's by a relative error of at most 0.025.
Values may be sent and summed in bfloat16 or wider, within the bound.
No kernel may reach another device: no remote copies, remote signals or barrier semaphores. Data moves between devices by JAX's collectives and lax.ppermute only.
A program may use at most 256 MiB of HBM per device.

v0:
```python
import math
import jax
import jax.numpy as jnp
from jax import lax
from jax.sharding import PartitionSpec as P

D = 2048
HEAD_K = 512
HEAD_V = 512
BLOCK = 64
SLOT = 1280
EPSILON = 1e-06
HIGHEST = lax.Precision.HIGHEST


def for_sending(x):

    def short(part):
        return part.astype(jnp.bfloat16) if part.dtype == jnp.float32 else part

    return jax.tree.map(short, x)


def product(left, right):
    return jnp.dot(left, right, preferred_element_type=jnp.float32)


def contract_rows(left, right):
    return lax.dot_general(
        left, right, (((0,), (0,)), ((), ())), preferred_element_type=jnp.float32
    )


def contract_cols(left, right):
    return lax.dot_general(
        left, right, (((1,), (1,)), ((), ())), preferred_element_type=jnp.float32
    )


def gla_sequence(queries, key_rows, value_rows, decays):
    block_count = queries.shape[0] // BLOCK
    key_extent = queries.shape[1]
    value_extent = value_rows.shape[1]
    query_blocks = queries.reshape(block_count, BLOCK, key_extent)
    key_blocks = key_rows.reshape(block_count, BLOCK, key_extent)
    value_blocks = value_rows.reshape(block_count, BLOCK, value_extent)
    decay_blocks = decays.reshape(block_count, BLOCK, key_extent)
    running = jnp.cumsum(decay_blocks, axis=1)
    ending = running[:, -1:, :]
    query_fade = query_blocks * jnp.exp(running)
    key_grow = key_blocks * jnp.exp(-running)
    key_final = key_blocks * jnp.exp(ending - running)
    causal = jnp.tril(jnp.ones((BLOCK, BLOCK), jnp.float32))
    scores = jnp.einsum("bik,bjk->bij", query_fade, key_grow, precision=HIGHEST) * causal
    within = jnp.einsum("bij,bjv->biv", scores, value_blocks, precision=HIGHEST)
    updates = jnp.einsum("bjk,bjv->bkv", key_final, value_blocks, precision=HIGHEST)
    fading = jnp.exp(ending[:, 0, :])

    def advance(carried, inputs_now):
        update_now, fade_now = inputs_now
        return (carried * fade_now[:, None] + update_now, carried)

    initial = jnp.zeros((key_extent, value_extent), jnp.float32)
    _, earlier = lax.scan(advance, initial, (updates, fading))
    across = jnp.einsum("bik,bkv->biv", query_fade, earlier, precision=HIGHEST)
    return (within + across).reshape(block_count * BLOCK, value_extent)


def row_total(partial_value):
    return lax.psum(partial_value, "row")


def norm_forward(values, gains, extent):
    summed = row_total(jnp.sum(values * values, axis=1))
    factor = lax.rsqrt(summed / extent + EPSILON)
    return (values * factor[:, None] * gains, factor)


def norm_backward(values, factor, gains, upstream, extent):
    weighted = upstream * gains
    inner_sum = row_total(jnp.sum(weighted * values, axis=1))
    grad_values = (
        factor[:, None] * weighted
        - values * (factor * factor * factor * inner_sum / extent)[:, None]
    )
    grad_gains = jnp.sum(upstream * values * factor[:, None], axis=0)
    return (grad_values, grad_gains)


def gather_tokens(tensor):
    return lax.all_gather(tensor, "col", axis=0, tiled=True)


def share_features(parts):
    return lax.psum_scatter(parts, "row", scatter_dimension=1, tiled=True)


def gather_features(parts):
    return jax.tree.map(
        lambda part, own: part.astype(own.dtype),
        lax.all_gather(for_sending(parts), "row", axis=1, tiled=True),
        parts,
    )


def reduce_tokens(builder, local_rows):
    return lax.psum_scatter(
        builder(jnp.int32(0), local_rows * lax.axis_size("col")),
        "col",
        scatter_dimension=0,
        tiled=True,
    )


def body(
    hidden_in,
    seq_lengths,
    gain_attn,
    w_query,
    w_key,
    w_value,
    w_outgate,
    rank_down,
    rank_up,
    decay_bias,
    gain_head,
    w_output,
    gain_ffn,
    w_gate,
    w_up,
    w_down,
    cotangent,
):
    local_rows = hidden_in.shape[0]
    col_index = lax.axis_index("col")
    row_index = lax.axis_index("row")
    group_rows = local_rows * lax.axis_size("col")
    key_share = HEAD_K // lax.axis_size("row")
    query_scale = 1.0 / math.sqrt(HEAD_K)
    places = jnp.arange(group_rows)
    owners = (places // SLOT)[:, None] == jnp.arange(seq_lengths.shape[0])[None, :]
    limits = jnp.sum(jnp.where(owners, seq_lengths[None, :], 0), axis=1)
    valid_group = (places % SLOT < limits).astype(jnp.float32)
    valid_here = lax.dynamic_slice_in_dim(valid_group, col_index * local_rows, local_rows)
    gain_attn_f = gain_attn.astype(jnp.float32)
    gain_head_f = gain_head.astype(jnp.float32)
    gain_ffn_f = gain_ffn.astype(jnp.float32)
    residual_in = hidden_in.astype(jnp.float32)
    normed_one, factor_one = norm_forward(residual_in, gain_attn_f, D)
    normed_one_low = normed_one.astype(jnp.bfloat16)
    tokens_one = gather_tokens(normed_one_low)
    query_part, key_part, outgate_share = share_features(
        (product(tokens_one, w_query), product(tokens_one, w_key), product(tokens_one, w_outgate))
    )
    value_full, rank_full = lax.psum(
        (product(tokens_one, w_value), product(tokens_one, rank_down)), "row"
    )
    query_low = query_part.astype(jnp.bfloat16)
    key_low = key_part.astype(jnp.bfloat16)
    value_low = value_full.astype(jnp.bfloat16)
    rank_low = rank_full.astype(jnp.bfloat16)
    rank_cols = lax.dynamic_slice_in_dim(rank_up, row_index * key_share, key_share, 1)
    bias_cols = lax.dynamic_slice_in_dim(decay_bias, row_index * key_share, key_share, 0)
    decay_logits = product(rank_low, rank_cols) + bias_cols
    decays = jax.nn.log_sigmoid(decay_logits) / 16.0

    def reshape_slots(tensor):
        return tensor.reshape(seq_lengths.shape[0], SLOT, tensor.shape[1])

    def attend(queries, key_rows, value_rows, decay_rows):
        mixed_slots = jax.vmap(gla_sequence)(
            reshape_slots(queries),
            reshape_slots(key_rows),
            reshape_slots(value_rows),
            reshape_slots(decay_rows),
        )
        return mixed_slots.reshape(group_rows, value_rows.shape[1])

    mixed_part, attend_back = jax.vjp(
        attend,
        query_low.astype(jnp.float32) * query_scale,
        key_low.astype(jnp.float32),
        value_low.astype(jnp.float32),
        decays,
    )
    mixed_share = share_features(mixed_part)
    normed_head, factor_head = norm_forward(mixed_share, gain_head_f, HEAD_V)
    outgate_sig = jax.nn.sigmoid(outgate_share)
    outgate_act = outgate_share * outgate_sig
    gated_share = (normed_head * outgate_act).astype(jnp.bfloat16)
    gated_all = gather_features(gated_share)

    def attn_rows(first_row, row_count):
        return product(gated_all, w_output)

    attn_out = reduce_tokens(attn_rows, local_rows)
    residual_mid = residual_in + attn_out
    normed_two, factor_two = norm_forward(residual_mid, gain_ffn_f, D)
    normed_two_low = normed_two.astype(jnp.bfloat16)
    tokens_two = gather_tokens(normed_two_low)
    gate_pre, up_pre = share_features((product(tokens_two, w_gate), product(tokens_two, w_up)))
    swish_sig = jax.nn.sigmoid(gate_pre)
    swish_out = gate_pre * swish_sig
    hidden_share = (swish_out * up_pre).astype(jnp.bfloat16)
    hidden_all = gather_features(hidden_share)

    def ffn_rows(first_row, row_count):
        return product(hidden_all, w_down)

    ffn_out = reduce_tokens(ffn_rows, local_rows)
    block_out = (valid_here[:, None] * (residual_mid + ffn_out)).astype(jnp.bfloat16)
    upstream = valid_here[:, None] * cotangent.astype(jnp.float32)
    ffn_grad_all = gather_tokens(upstream.astype(jnp.bfloat16))
    hidden_grad = share_features(contract_cols(ffn_grad_all, w_down))
    grad_down = contract_rows(hidden_all, ffn_grad_all)
    swish_slope = swish_sig * (1.0 + gate_pre * (1.0 - swish_sig))
    gate_grad = (hidden_grad * up_pre * swish_slope).astype(jnp.bfloat16)
    up_grad = (hidden_grad * swish_out).astype(jnp.bfloat16)
    gate_grad_all, up_grad_all = gather_features((gate_grad, up_grad))
    grad_gate = contract_rows(tokens_two, gate_grad_all)
    grad_up = contract_rows(tokens_two, up_grad_all)

    def norm_two_rows(first_row, row_count):
        return contract_cols(gate_grad_all, w_gate) + contract_cols(up_grad_all, w_up)

    normed_two_grad = reduce_tokens(norm_two_rows, local_rows)
    mid_part, gain_ffn_grad = norm_backward(
        residual_mid, factor_two, gain_ffn_f, normed_two_grad, D
    )
    mid_grad = upstream + mid_part
    attn_grad_all = gather_tokens(mid_grad.astype(jnp.bfloat16))
    grad_output = contract_rows(gated_all, attn_grad_all)
    gated_grad = share_features(contract_cols(attn_grad_all, w_output))
    head_grad = gated_grad * outgate_act
    outgate_slope = outgate_sig * (1.0 + outgate_share * (1.0 - outgate_sig))
    outgate_grad = (gated_grad * normed_head * outgate_slope).astype(jnp.bfloat16)
    mixed_grad, gain_head_grad = norm_backward(
        mixed_share, factor_head, gain_head_f, head_grad, HEAD_V
    )
    mixed_grad_all, outgate_grad_all = gather_features(
        (mixed_grad.astype(jnp.bfloat16), outgate_grad)
    )
    scaled_grad, key_grad, value_part, decay_grad = attend_back(mixed_grad_all.astype(jnp.float32))
    value_grad = lax.psum(value_part, "row").astype(jnp.bfloat16)
    query_grad = (scaled_grad * query_scale).astype(jnp.bfloat16)
    key_grad_low = key_grad.astype(jnp.bfloat16)
    logit_grad = decay_grad * jax.nn.sigmoid(-decay_logits) / 16.0
    rank_up_part = lax.dot_general(
        rank_low.astype(jnp.float32),
        logit_grad,
        (((0,), (0,)), ((), ())),
        precision=HIGHEST,
        preferred_element_type=jnp.float32,
    )
    rank_up_grad = lax.dynamic_update_slice_in_dim(
        jnp.zeros(rank_up.shape, jnp.float32), rank_up_part, row_index * key_share, 1
    )
    bias_grad = lax.dynamic_update_slice_in_dim(
        jnp.zeros(decay_bias.shape, jnp.float32),
        jnp.sum(logit_grad, axis=0),
        row_index * key_share,
        0,
    )
    rank_term = lax.dot_general(
        logit_grad,
        rank_cols.astype(jnp.float32),
        (((1,), (1,)), ((), ())),
        precision=HIGHEST,
        preferred_element_type=jnp.float32,
    )
    rank_grad = lax.psum(rank_term, ("row", "col")).astype(jnp.bfloat16)
    query_grad_all, key_grad_all = gather_features((query_grad, key_grad_low))
    grad_query = contract_rows(tokens_one, query_grad_all)
    grad_key = contract_rows(tokens_one, key_grad_all)
    grad_value = contract_rows(tokens_one, value_grad)
    grad_outgate = contract_rows(tokens_one, outgate_grad_all)
    grad_rank_down = contract_rows(tokens_one, rank_grad)

    def norm_one_rows(first_row, row_count):
        summed = contract_cols(query_grad_all, w_query)
        summed = summed + contract_cols(key_grad_all, w_key)
        summed = summed + contract_cols(value_grad, w_value)
        summed = summed + contract_cols(outgate_grad_all, w_outgate)
        return summed

    normed_one_grad = reduce_tokens(norm_one_rows, local_rows)
    own_rank = lax.dynamic_slice_in_dim(rank_grad, col_index * local_rows, local_rows, 0)
    normed_one_grad = normed_one_grad + contract_cols(own_rank, rank_down)
    input_part, gain_attn_grad = norm_backward(
        residual_in, factor_one, gain_attn_f, normed_one_grad, D
    )
    grad_input = mid_grad + input_part
    weights_summed = (
        lax.psum(grad_query.astype(jnp.bfloat16), "dp").astype(jnp.float32),
        lax.psum(grad_key.astype(jnp.bfloat16), "dp").astype(jnp.float32),
        lax.psum(grad_value.astype(jnp.bfloat16), "dp").astype(jnp.float32),
        lax.psum(grad_outgate.astype(jnp.bfloat16), "dp").astype(jnp.float32),
        lax.psum(grad_rank_down.astype(jnp.bfloat16), "dp").astype(jnp.float32),
        lax.psum(grad_output.astype(jnp.bfloat16), "dp").astype(jnp.float32),
        lax.psum(grad_gate.astype(jnp.bfloat16), "dp").astype(jnp.float32),
        lax.psum(grad_up.astype(jnp.bfloat16), "dp").astype(jnp.float32),
        lax.psum(grad_down.astype(jnp.bfloat16), "dp").astype(jnp.float32),
    )
    gains_summed = lax.psum((gain_attn_grad, gain_head_grad, gain_ffn_grad), ("dp", "col"))
    decay_summed = (
        lax.psum(rank_up_grad.astype(jnp.bfloat16), ("dp", "row")).astype(jnp.float32),
        lax.psum(bias_grad.astype(jnp.bfloat16), ("dp", "row")).astype(jnp.float32),
    )
    return (
        block_out,
        grad_input,
        gains_summed[0],
        weights_summed[0],
        weights_summed[1],
        weights_summed[2],
        weights_summed[3],
        weights_summed[4],
        decay_summed[0],
        decay_summed[1],
        gains_summed[1],
        weights_summed[5],
        gains_summed[2],
        weights_summed[6],
        weights_summed[7],
        weights_summed[8],
    )


def solution(mesh):
    placed = (
        P(("dp", "col"), "row"),
        P("dp"),
        P("row"),
        P("row", "col"),
        P("row", "col"),
        P("row", "col"),
        P("row", "col"),
        P("row", None),
        P(None, "col"),
        P("col"),
        P("row"),
        P("col", "row"),
        P("row"),
        P("row", "col"),
        P("row", "col"),
        P("col", "row"),
        P(("dp", "col"), "row"),
    )
    return jax.shard_map(
        body,
        mesh=mesh,
        in_specs=placed,
        out_specs=(
            P(("dp", "col"), "row"),
            P(("dp", "col"), "row"),
            P("row"),
            P("row", "col"),
            P("row", "col"),
            P("row", "col"),
            P("row", "col"),
            P("row", None),
            P(None, "col"),
            P("col"),
            P("row"),
            P("col", "row"),
            P("row"),
            P("row", "col"),
            P("row", "col"),
            P("col", "row"),
        ),
        check_vma=False,
    )
```

profile of v0, /device:TPU:0, one launch (start us, length us, event | category | flops | bytes accessed | tf_op | source)
XLA Modules:
  0.0 2069.8 jit_solution(14009256386679125751)
XLA Ops:
  8.7 5.8 psum.168
  18.1 56.7 %all-gather.13.cloned.1.call-done = bf16[1280,1024]{1,0:T(8,128)(2,1)} async-done(((bf16[320,1024]{1,0:T(8,128)(2,1)}), bf16[1280,1024]{1,0:T(8,128)(2,1)}) %all-gather.13.cloned.1.call-update) | async-done | bytes 2621456 | tf_op jit(solution)/shard_map/all_gather | solution.py:91
  74.8 5.0 fusion.76
  79.9 5.0 fusion.78
  85.7 5.2 fusion.79
  91.7 112.6 %all-reduce.10 = (bf16[1280,16]{0,1:T(8,128)(2,1)}, bf16[1280,512]{1,0:T(8,128)(2,1)}) all-reduce(f32[1280,16]{0,1:T(8,128)S(1)} %fusion.77, f32[1280,512]{1,0:T(8,128)} %fusion.79), channel_id=1, replica_groups=mesh['dp'=4,'row'=2,'col'=4] {'row'}, use_global_device_ids=true, to_apply=%region_3.4 | all-reduce | flops 675840 | bytes 4055040 | tf_op jit(solution)/shard_map/psum | solution.py:155
  215.7 7.2 convolution_bitcast_fusion.1
  222.9 5.2 broadcast.104.clone
  228.1 51.8 %while.34 = (s32[]{:T(128)}, f32[1,256,512]{2,1,0:T(8,128)S(1)}, f32[20,1,256,512]{3,2,1,0:T(8,128)}, f32[20,1,256,1]{2,3,1,0:T(1,128)}, f32[20,1,256]{2,1,0:T(1...) while((s32[]{:T(128)}, f32[1,256,512]{2,1,0:T(8,128)S(1)}, ...), condition=%wide.region_8.9_spmd.clone, body=%wide.region_7.8_spmd.clone.sunk | while | flops 524291 | bytes 2627688 | solution.py:64
  285.1 12.0 fusion.10
  297.6 5.0 fusion.81
  303.3 32.6 %reduce-scatter.17.cloned.1.call-done = f32[1280,256]{1,0:T(8,128)} async-done(((f32[1280,512]{1,0:T(8,128)}), f32[1280,256]{1,0:T(8,128)}) %reduce-scatter.17.cloned.1.call-update) | async-done | bytes 1310736 | tf_op jit(solution)/shard_map/reduce_scatter | solution.py:95
  337.5 5.0 psum.171
  342.5 33.8 %reduce-scatter.19.cloned.1.call-done = f32[1280,256]{1,0:T(8,128)} async-done(((f32[1280,512]{1,0:T(8,128)}), f32[1280,256]{1,0:T(8,128)}) %reduce-scatter.19.cloned.1.call-update) | async-done | bytes 1310736 | tf_op jit(solution)/shard_map/reduce_scatter | solution.py:95
  379.4 24.3 %all-gather.15.cloned.1.call-done = bf16[1280,512]{1,0:T(8,128)(2,1)} async-done(((bf16[1280,256]{1,0:T(8,128)(2,1)}), bf16[1280,512]{1,0:T(8,128)(2,1)}) %all-gather.15.cloned.1.call-update) | async-done | bytes 1310736 | tf_op jit(solution)/shard_map/all_gather | solution.py:101
  403.7 5.5 fusion.82
  414.1 89.1 %reduce-scatter.21.cloned.1.call-done = f32[320,1024]{1,0:T(8,128)} async-done(((f32[1280,1024]{1,0:T(8,128)}), f32[320,1024]{1,0:T(8,128)}) %reduce-scatter.21.cloned.1.call-update) | async-done | bytes 1310736 | tf_op jit(solution)/shard_map/reduce_scatter | solution.py:107
  506.3 5.0 psum.172
  514.4 46.3 %all-gather.21.cloned.1.call-done = bf16[1280,1024]{1,0:T(8,128)(2,1)} async-done(((bf16[320,1024]{1,0:T(8,128)(2,1)}), bf16[1280,1024]{1,0:T(8,128)(2,1)}) %all-gather.21.cloned.1.call-update) | async-done | bytes 2621456 | tf_op jit(solution)/shard_map/all_gather | solution.py:91
  560.7 9.5 fusion.86
  570.2 46.2 %all-gather.17.cloned.1.call-done = bf16[1280,1024]{1,0:T(8,128)(2,1)} async-done(((bf16[320,1024]{1,0:T(8,128)(2,1)}), bf16[1280,1024]{1,0:T(8,128)(2,1)}) %all-gather.17.cloned.1.call-update) | async-done | bytes 2621456 | tf_op jit(solution)/shard_map/all_gather | solution.py:91
  616.4 8.3 fusion.83
  624.8 9.5 fusion.84
  634.4 70.0 %reduce-scatter.29.cloned.1.call-done = f32[1280,704]{0,1:T(8,128)} async-done(((f32[1280,1408]{0,1:T(8,128)}), f32[1280,704]{0,1:T(8,128)}) %reduce-scatter.29.cloned.1.call-update) | async-done | bytes 3604496 | tf_op jit(solution)/shard_map/reduce_scatter | solution.py:95
  704.4 89.5 %reduce-scatter.23.cloned.1.call-done = f32[1280,704]{0,1:T(8,128)} async-done(((f32[1280,1408]{0,1:T(8,128)}), f32[1280,704]{0,1:T(8,128)}) %reduce-scatter.23.cloned.1.call-update) | async-done | bytes 3604496 | tf_op jit(solution)/shard_map/reduce_scatter | solution.py:95
  793.9 89.2 %reduce-scatter.25.cloned.1.call-done = f32[1280,704]{0,1:T(8,128)} async-done(((f32[1280,1408]{0,1:T(8,128)}), f32[1280,704]{0,1:T(8,128)}) %reduce-scatter.25.cloned.1.call-update) | async-done | bytes 3604496 | tf_op jit(solution)/shard_map/reduce_scatter | solution.py:95
  883.1 6.6 multiply_convert_fusion
  891.1 48.9 %all-gather.23.cloned.1.call-done = bf16[1280,1408]{0,1:T(8,128)(2,1)} async-done(((bf16[1280,704]{0,1:T(8,128)(2,1)}), bf16[1280,1408]{0,1:T(8,128)(2,1)}) %all-gather.23.cloned.1.call-update) | async-done | bytes 3604496 | tf_op jit(solution)/shard_map/all_gather | solution.py:101
  940.0 8.0 fusion.87
  948.1 44.1 %all-gather.25.cloned.1.call-done = bf16[1280,1408]{0,1:T(8,128)(2,1)} async-done(((bf16[1280,704]{0,1:T(8,128)(2,1)}), bf16[1280,1408]{0,1:T(8,128)(2,1)}) %all-gather.25.cloned.1.call-update) | async-done | bytes 3604496 | tf_op jit(solution)/shard_map/all_gather | solution.py:101
  992.2 11.2 convolution_add_fusion
  1003.4 40.9 %all-gather.19.cloned.1.call-done = bf16[1280,1408]{0,1:T(8,128)(2,1)} async-done(((bf16[1280,704]{0,1:T(8,128)(2,1)}), bf16[1280,1408]{0,1:T(8,128)(2,1)}) %all-gather.19.cloned.1.call-update) | async-done | bytes 3604496 | tf_op jit(solution)/shard_map/all_gather | solution.py:101
  1044.4 8.0 fusion.85
  1052.5 88.5 %reduce-scatter.31.cloned.1.call-done = f32[320,1024]{1,0:T(8,128)} async-done(((f32[1280,1024]{1,0:T(8,128)}), f32[320,1024]{1,0:T(8,128)}) %reduce-scatter.31.cloned.1.call-update) | async-done | bytes 1310736 | tf_op jit(solution)/shard_map/reduce_scatter | solution.py:107
  1143.4 4.9 psum.173
  1148.3 89.8 %reduce-scatter.27.cloned.1.call-done = f32[320,1024]{1,0:T(8,128)} async-done(((f32[1280,1024]{1,0:T(8,128)}), f32[320,1024]{1,0:T(8,128)}) %reduce-scatter.27.cloned.1.call-update) | async-done | bytes 1310736 | tf_op jit(solution)/shard_map/reduce_scatter | solution.py:107
  1241.6 55.5 %all-gather.27.cloned.1.call-done = bf16[1280,1024]{1,0:T(8,128)(2,1)} async-done(((bf16[320,1024]{1,0:T(8,128)(2,1)}), bf16[1280,1024]{1,0:T(8,128)(2,1)}) %all-gather.27.cloned.1.call-update) | async-done | bytes 2621456 | tf_op jit(solution)/shard_map/all_gather | solution.py:91
  1297.0 5.1 fusion.88
  1303.8 7.8 convolution_convert_fusion.1
  1311.6 5.7 convolution_convert_fusion.2
  1317.3 21.3 %reduce-scatter.33.cloned.1.call-done = f32[1280,256]{1,0:T(8,128)} async-done(((f32[1280,512]{1,0:T(8,128)}), f32[1280,256]{1,0:T(8,128)}) %reduce-scatter.33.cloned.1.call-update) | async-done | bytes 1310736 | tf_op jit(solution)/shard_map/reduce_scatter | solution.py:95
  1342.2 5.0 psum.174
  1350.0 8.5 convolution_convert_fusion
  1361.4 12.9 all-gather.29.cloned.1.call-done
  1374.3 9.8 convolution_bitcast_fusion
  1384.1 10.8 fusion.5
  1397.5 5.3 broadcast.104
  1402.9 136.7 %while.35 = (s32[]{:T(128)}, f32[1,256,512]{2,1,0:T(8,128)S(1)}, f32[20,1,256,512]{3,2,1,0:T(8,128)}, f32[20,1,256]{2,1,0:T(1,128)S(1)}, f32[20,1,256,512]{2,3,0...) while((s32[]{:T(128)}, f32[1,256,512]{2,1,0:T(8,128)S(1)}, ...), condition=%wide.region_28.29_spmd.clone, body=%wide.region_26.28_spmd.clone.sunk | while | flops 786180 | bytes 5249168 | solution.py:64
  1539.7 10.9 fusion.50
  1550.6 9.8 fusion.13
  1568.0 78.9 %all-reduce.11 = bf16[1280,512]{1,0:T(8,128)(2,1)} all-reduce(f32[1280,512]{1,0:T(8,128)} %bitcast.223), channel_id=1, replica_groups=mesh['dp'=4,'row'=2,'col'=4] {'row'}, use_global_device_ids=true, to_apply=%region_29.30 | all-reduce | flops 655360 | bytes 3932160 | tf_op jit(solution)/shard_map/psum | solution.py:244
  1647.1 3.8 convolution_convert_fusion.5
  1654.7 3.9 convolution_convert_fusion.6
  1658.6 13.4 all-gather.31.cloned.1.call-done
  1672.0 3.8 convolution_convert_fusion.7
  1683.8 4.2 add_add_fusion
  1694.1 23.7 %all-reduce.3 = (bf16[16,512]{1,0:T(8,128)(2,1)S(1)}, bf16[512]{0:T(512)(128)(2,1)S(1)}) all-reduce(bf16[16,512]{1,0:T(8,128)(2,1)S(1)} %convolution_dynamic-update-slice_fusion, bf16[512]{0:T(512)(128)(2,1)S(1)} %dynamic_update_slice.34), channel_id=1, replica_groups=mesh['dp'=4,'row'=2,'col'=4] {'dp','row'}, use_global_device_ids=true, to_apply=%region_43.44 | all-reduce | flops 8704 | bytes 34816 | tf_op jit(solution)/shard_map/psum | solution.py:306
  1719.8 38.8 %psum.176 = bf16[1280,16]{0,1:T(8,128)(2,1)S(1)} all-reduce(f32[1280,16]{0,1:T(8,128)S(1)} %fusion.60), channel_id=1, replica_groups=mesh['dp'=4,'row'=2,'col'=4] {'row','col'}, use_global_device_ids=true, to_apply=%region_33.34 | all-reduce | flops 20480 | bytes 122880 | tf_op jit(solution)/shard_map/psum | solution.py:271
  1760.8 12.6 psum.183
  1774.0 147.4 %all-reduce.9.cloned.1.call-done = (bf16[1024,512]{1,0:T(8,128)(2,1)}, bf16[1024,512]{1,0:T(8,128)(2,1)}, bf16[1024,512]{1,0:T(8,128)(2,1)}, bf16[1024,512]{1,0:...) async-done(((bf16[1024,512]{1,0:T(8,128)(2,1)}, bf16[1024,512]{1,0:T(8,128)(2,1)}, ...) | async-done | bytes 13893648 | tf_op jit(solution)/shard_map/psum | solution.py:294
  1921.4 4.9 convert_element_type.203
  1940.8 76.9 %reduce-scatter.35.cloned.1.call-done = f32[320,1024]{1,0:T(8,128)} async-done(((f32[1280,1024]{1,0:T(8,128)}), f32[320,1024]{1,0:T(8,128)}) %reduce-scatter.35.cloned.1.call-update) | async-done | bytes 1310736 | tf_op jit(solution)/shard_map/reduce_scatter | solution.py:107
  2020.7 4.9 psum.177
  2025.7 33.8 %all-reduce.1 = (f32[1024]{0:T(1024)}, f32[256]{0:T(256)}, f32[1024]{0:T(1024)}) all-reduce(f32[1024]{0:T(1024)S(1)} %get-tuple-element.257, f32[256]{0:T(256)S(1)} %copy-done.72, f32[1024]{0:T(1024)S(1)} %copy-done.67), channel_id=1, replica_groups=mesh['dp'=4,'row'=2,'col'=4] {'dp','col'}, use_global_device_ids=true, to_apply=%region_37.38 | all-reduce | flops 2304 | bytes 18432 | tf_op jit(solution)/shard_map/psum | solution.py:304
  (490 shorter events, 298.9 us)
Async XLA Ops:
  7.2 609.2 %copy-start = (bf16[1024,1408]{1,0:T(8,128)(2,1)S(1)}, bf16[1024,1408]{1,0:T(8,128)(2,1)}, u32[]{:S(2)}) copy-start(bf16[1024,1408]{1,0:T(8,128)(2,1)} %param.34) | copy-start | bytes 8650756
  7.2 67.6 %all-gather.13.cloned.1.call-start = ((), (), s32[]{:S(2)}) async-start(), calls=%async_computation.12 | async-start | bytes 3276800 | tf_op jit(solution)/shard_map/all_gather | solution.py:91
  14.5 65.3 %copy-start.63 = (f32[320]{0:T(512)}, f32[320]{0:T(512)S(1)}, u32[]{:S(2)}) copy-start(f32[320]{0:T(512)S(1)} %psum.168) | copy-start | bytes 3844
  18.0 191.0 %reduce-scatter.13.cloned.1.call-start = ((), (), s32[]{:S(2)}) async-start(), calls=%async_computation.13 | async-start | bytes 3932160 | tf_op jit(solution)/shard_map/reduce_scatter | solution.py:95
  79.8 133.7 %reduce-scatter.15.cloned.1.call-start = ((), (), s32[]{:S(2)}) async-start(), calls=%async_computation.14 | async-start | bytes 3932160 | tf_op jit(solution)/shard_map/reduce_scatter | solution.py:95
  84.9 251.0 %reduce-scatter.17.cloned.1.call-start = ((), (), s32[]{:S(2)}) async-start(), calls=%async_computation.15 | async-start | bytes 3932160 | tf_op jit(solution)/shard_map/reduce_scatter | solution.py:95
  85.7 194.2 %copy-start.48 = (f32[64,64]{1,0:T(8,128)}, f32[64,64]{1,0:T(8,128)S(1)}, u32[]{:S(2)}) copy-start(f32[64,64]{1,0:T(8,128)S(1)} %fusion.52) | copy-start | bytes 49156
  91.7 112.6 %copy-start.70 = (bf16[16,512]{1,0:T(8,128)(2,1)S(1)}, bf16[16,512]{1,0:T(8,128)(2,1)}, u32[]{:S(2)}) copy-start(bf16[16,512]{1,0:T(8,128)(2,1)} %param.29) | copy-start | bytes 49156
  297.1 79.2 %reduce-scatter.19.cloned.1.call-start = ((), (), s32[]{:S(2)}) async-start(), calls=%async_computation.16 | async-start | bytes 3932160 | tf_op jit(solution)/shard_map/reduce_scatter | solution.py:95
  302.7 101.0 %all-gather.15.cloned.1.call-start = ((), (), s32[]{:S(2)}) async-start(), calls=%async_computation.17 | async-start | bytes 1966080 | tf_op jit(solution)/shard_map/all_gather | solution.py:101
  303.3 76.0 %copy-start.68 = (f32[256]{0:T(256)}, f32[256]{0:T(256)S(1)}, u32[]{:S(2)}) copy-start(f32[256]{0:T(256)S(1)} %convert_element_type.167) | copy-start | bytes 3076
  379.3 123.8 %reduce-scatter.21.cloned.1.call-start = ((), (), s32[]{:S(2)}) async-start(), calls=%async_computation.18 | async-start | bytes 6553600 | tf_op jit(solution)/shard_map/reduce_scatter | solution.py:107
  409.2 93.9 %copy-start.18 = (bf16[320,1024]{1,0:T(8,128)(2,1)S(1)}, bf16[320,1024]{1,0:T(8,128)(2,1)}, u32[]{:S(2)}) copy-start(bf16[320,1024]{1,0:T(8,128)(2,1)} %param.21) | copy-start | bytes 1966084
  409.2 151.4 %all-gather.21.cloned.1.call-start = ((), (), s32[]{:S(2)}) async-start(), calls=%async_computation.24 | async-start | bytes 3276800 | tf_op jit(solution)/shard_map/all_gather | solution.py:91
  412.7 203.7 %all-gather.17.cloned.1.call-start = ((), (), s32[]{:S(2)}) async-start(), calls=%async_computation.19 | async-start | bytes 3276800 | tf_op jit(solution)/shard_map/all_gather | solution.py:91
  514.4 190.0 %reduce-scatter.29.cloned.1.call-start = ((), (), s32[]{:S(2)}) async-start(), calls=%async_computation.25 | async-start | bytes 10813440 | tf_op jit(solution)/shard_map/reduce_scatter | solution.py:95
  570.2 223.7 %reduce-scatter.23.cloned.1.call-start = ((), (), s32[]{:S(2)}) async-start(), calls=%async_computation.20 | async-start | bytes 10813440 | tf_op jit(solution)/shard_map/reduce_scatter | solution.py:95
  624.7 258.3 %reduce-scatter.25.cloned.1.call-start = ((), (), s32[]{:S(2)}) async-start(), calls=%async_computation.21 | async-start | bytes 10813440 | tf_op jit(solution)/shard_map/reduce_scatter | solution.py:95
  634.3 305.7 %all-gather.23.cloned.1.call-start = ((), (), s32[]{:S(2)}) async-start(), calls=%async_computation.26 | async-start | bytes 5406720 | tf_op jit(solution)/shard_map/all_gather | solution.py:101
  889.7 102.5 %all-gather.25.cloned.1.call-start = ((), (), s32[]{:S(2)}) async-start(), calls=%async_computation.27 | async-start | bytes 5406720 | tf_op jit(solution)/shard_map/all_gather | solution.py:101
  890.3 154.1 %all-gather.19.cloned.1.call-start = ((), (), s32[]{:S(2)}) async-start(), calls=%async_computation.22 | async-start | bytes 5406720 | tf_op jit(solution)/shard_map/all_gather | solution.py:101
  890.9 250.1 %reduce-scatter.31.cloned.1.call-start = ((), (), s32[]{:S(2)}) async-start(), calls=%async_computation.28 | async-start | bytes 6553600 | tf_op jit(solution)/shard_map/reduce_scatter | solution.py:107
  1003.4 41.0 %copy-start.75 = (bf16[1408,1024]{1,0:T(8,128)(2,1)S(1)}, bf16[1408,1024]{1,0:T(8,128)(2,1)}, u32[]{:S(2)}) copy-start(bf16[1408,1024]{1,0:T(8,128)(2,1)} %param.36) | copy-start | bytes 8650756
  1003.4 234.8 %reduce-scatter.27.cloned.1.call-start = ((), (), s32[]{:S(2)}) async-start(), calls=%async_computation.23 | async-start | bytes 6553600 | tf_op jit(solution)/shard_map/reduce_scatter | solution.py:107
  1052.4 88.6 %copy-start.17 = (f32[320,1024]{1,0:T(8,128)S(1)}, f32[320,1024]{1,0:T(8,128)}, u32[]{:S(2)}) copy-start(f32[320,1024]{1,0:T(8,128)} %get-tuple-element.305) | copy-start | bytes 3932164
  1052.4 88.6 %copy-start.53 = (f32[1024]{0:T(1024)S(1)}, f32[1024]{0:T(1024)}, u32[]{:S(2)}) copy-start(f32[1024]{0:T(1024)} %convert_element_type.169) | copy-start | bytes 12292
  1052.4 88.6 %copy-start.58 = (f32[320]{0:T(512)S(1)}, f32[320]{0:T(512)}, u32[]{:S(2)}) copy-start(f32[320]{0:T(512)} %copy-done.57) | copy-start | bytes 3844
  1052.4 95.9 %copy-start.66 = (f32[320]{0:T(512)S(1)}, f32[320]{0:T(512)}, u32[]{:S(2)}) copy-start(f32[320]{0:T(512)} %copy-done.65) | copy-start | bytes 3844
  1052.4 185.7 %copy-start.34 = (bf16[320,1024]{1,0:T(8,128)(2,1)S(1)}, bf16[320,1024]{1,0:T(8,128)(2,1)}, u32[]{:S(2)}) copy-start(bf16[320,1024]{1,0:T(8,128)(2,1)} %param.37) | copy-start | bytes 1966084
  1052.4 185.7 %copy-start.62 = (f32[320]{0:T(512)S(1)}, f32[320]{0:T(512)}, u32[]{:S(2)}) copy-start(f32[320]{0:T(512)} %copy-done.61) | copy-start | bytes 3844
  1052.5 244.5 %all-gather.27.cloned.1.call-start = ((), (), s32[]{:S(2)}) async-start(), calls=%async_computation.29 | async-start | bytes 3276800 | tf_op jit(solution)/shard_map/all_gather | solution.py:91
  1141.0 97.1 %copy-start.30 = (f32[320,1024]{1,0:T(8,128)S(1)}, f32[320,1024]{1,0:T(8,128)}, u32[]{:S(2)}) copy-start(f32[320,1024]{1,0:T(8,128)} %reduce-scatter.31.cloned.1.call-done) | copy-start | bytes 3932164
  1241.5 97.1 %reduce-scatter.33.cloned.1.call-start = ((), (), s32[]{:S(2)}) async-start(), calls=%async_computation.30 | async-start | bytes 3932160 | tf_op jit(solution)/shard_map/reduce_scatter | solution.py:95
  1302.1 72.2 %all-gather.29.cloned.1.call-start = ((), (), s32[]{:S(2)}) async-start(), calls=%async_computation.31 | async-start | bytes 1966080 | tf_op jit(solution)/shard_map/all_gather | solution.py:101
  1303.8 7.8 copy-start.77
  1311.6 27.0 %copy-start.16 = (f32[1280,256]{1,0:T(8,128)S(1)}, f32[1280,256]{1,0:T(8,128)}, u32[]{:S(2)}) copy-start(f32[1280,256]{1,0:T(8,128)} %reduce-scatter.17.cloned.1.call-done) | copy-start | bytes 3932164
  1311.6 27.0 %copy-start.22 = (f32[1280,256]{1,0:T(8,128)S(1)}, f32[1280,256]{1,0:T(8,128)}, u32[]{:S(2)}) copy-start(f32[1280,256]{1,0:T(8,128)} %reduce-scatter.19.cloned.1.call-done) | copy-start | bytes 3932164
  1311.6 27.0 %copy-start.69 = (f32[256]{0:T(256)S(1)}, f32[256]{0:T(256)}, u32[]{:S(2)}) copy-start(f32[256]{0:T(256)} %copy-done.68) | copy-start | bytes 3076
  1349.9 8.5 copy-start.38
  1349.9 301.0 %all-gather.35.cloned.1.call-start = ((), (), s32[]{:S(2)}) async-start(), calls=%async_computation.34 | async-start | bytes 1966080 | tf_op jit(solution)/shard_map/all_gather | solution.py:101
  1350.0 8.5 copy-start.35
  1358.4 15.9 copy-start.9
  1361.0 293.8 %all-gather.33.cloned.1.call-start = ((), (), s32[]{:S(2)}) async-start(), calls=%async_computation.33 | async-start | bytes 1966080 | tf_op jit(solution)/shard_map/all_gather | solution.py:101
  1374.3 9.8 copy-start.14
  1384.1 10.8 copy-start.27
  1402.8 136.8 %copy-start.4 = (f32[1280,256]{1,0:T(8,128)S(1)}, f32[1280,256]{1,0:T(8,128)}, u32[]{:S(2)}) copy-start(f32[1280,256]{1,0:T(8,128)} %copy-done.3) | copy-start | bytes 3932164
  1402.9 136.8 %copy-start.7 = (f32[1,20,64,256]{3,2,1,0:T(8,128)S(1)}, f32[1,20,64,256]{3,2,1,0:T(8,128)}, u32[]{:S(2)}) copy-start(f32[1,20,64,256]{3,2,1,0:T(8,128)} %copy-done.5) | copy-start | bytes 3932164
  1402.9 136.8 %copy-start.47 = (f32[1,20,1,256]{3,1,2,0:T(8,128)S(1)}, f32[1,20,1,256]{3,1,2,0:T(8,128)}, u32[]{:S(2)}) copy-start(f32[1,20,1,256]{3,1,2,0:T(8,128)} %copy-done.46) | copy-start | bytes 61444
  1539.6 11.0 copy-start.2
  1550.6 9.9 copy-start.13
  1550.6 9.9 copy-start.15
  1550.6 9.9 copy-start.49
  1568.0 79.1 %copy-start.24 = (bf16[1280,1024]{1,0:T(8,128)(2,1)S(1)}, bf16[1280,1024]{1,0:T(8,128)(2,1)}, u32[]{:S(2)}) copy-start(bf16[1280,1024]{1,0:T(8,128)(2,1)} %all-gather.13.cloned.1.call-done) | copy-start | bytes 7864324
  1568.0 104.0 %all-gather.31.cloned.1.call-start = ((), (), s32[]{:S(2)}) async-start(), calls=%async_computation.32 | async-start | bytes 1966080 | tf_op jit(solution)/shard_map/all_gather | solution.py:101
  1647.0 274.4 %all-reduce.9.cloned.1.call-start = ((), (), s32[]{:S(2)}) async-start(), calls=%async_computation.36 | async-start | bytes 27787264 | tf_op jit(solution)/shard_map/psum | solution.py:294
  1675.9 341.8 %reduce-scatter.35.cloned.1.call-start = ((), (), s32[]{:S(2)}) async-start(), calls=%async_computation.35 | async-start | bytes 6553600 | tf_op jit(solution)/shard_map/reduce_scatter | solution.py:107
  1693.2 25.8 %copy-start.71 = (bf16[16,512]{1,0:T(8,128)(2,1)S(1)}, bf16[16,512]{1,0:T(8,128)(2,1)}, u32[]{:S(2)}) copy-start(bf16[16,512]{1,0:T(8,128)(2,1)} %param.29) | copy-start | bytes 49156
  1939.2 78.5 %copy-start.19 = (bf16[320,1024]{1,0:T(8,128)(2,1)S(1)}, bf16[320,1024]{1,0:T(8,128)(2,1)}, u32[]{:S(2)}) copy-start(bf16[320,1024]{1,0:T(8,128)(2,1)} %param.21) | copy-start | bytes 1966084
  1939.2 78.5 %copy-start.52 = (bf16[1024,16]{0,1:T(8,128)(2,1)S(1)}, bf16[1024,16]{0,1:T(8,128)(2,1)}, u32[]{:S(2)}) copy-start(bf16[1024,16]{0,1:T(8,128)(2,1)} %param.28) | copy-start | bytes 98308
  1939.2 78.5 %copy-start.55 = (f32[1024]{0:T(1024)S(1)}, f32[1024]{0:T(1024)}, u32[]{:S(2)}) copy-start(f32[1024]{0:T(1024)} %copy-done.54) | copy-start | bytes 12292
  1939.2 78.5 %copy-start.60 = (f32[320]{0:T(512)S(1)}, f32[320]{0:T(512)}, u32[]{:S(2)}) copy-start(f32[320]{0:T(512)} %copy-done.59) | copy-start | bytes 3844
  1940.8 84.9 %copy-start.64 = (f32[320]{0:T(512)S(1)}, f32[320]{0:T(512)}, u32[]{:S(2)}) copy-start(f32[320]{0:T(512)} %copy-done.63) | copy-start | bytes 3844
  1940.8 84.9 %copy-start.67 = (f32[1024]{0:T(1024)S(1)}, f32[1024]{0:T(1024)}, u32[]{:S(2)}) copy-start(f32[1024]{0:T(1024)} %get-tuple-element.255) | copy-start | bytes 12292
  1940.8 84.9 %copy-start.72 = (f32[256]{0:T(256)S(1)}, f32[256]{0:T(256)}, u32[]{:S(2)}) copy-start(f32[256]{0:T(256)} %get-tuple-element.253) | copy-start | bytes 3076
  (44 other events, 101.8 us)
Sparse Core Ops, SparseCore 0:
  18.1 56.6 all-gather.12
  79.9 53.6 reduce-scatter.12
  136.6 66.5 reduce-scatter.14
  297.3 38.6 reduce-scatter.16
  338.7 37.5 reduce-scatter.18
  379.4 24.1 all-gather.14
  409.3 93.7 reduce-scatter.20
  505.3 55.3 all-gather.20
  562.8 53.5 all-gather.16
  618.6 85.7 reduce-scatter.28
  706.8 87.0 reduce-scatter.22
  796.0 86.9 reduce-scatter.24
  889.9 50.1 all-gather.22
  942.1 50.0 all-gather.24
  994.2 50.0 all-gather.18
  1047.2 93.7 reduce-scatter.30
  1143.8 94.2 reduce-scatter.26
  1241.6 55.3 all-gather.26
  1302.2 36.3 reduce-scatter.32
  1350.0 24.2 all-gather.28
  1376.4 24.2 all-gather.34
  1568.1 38.4 all-gather.32
  1647.1 24.8 all-gather.30
  1676.2 245.1 all-reduce.8
  1923.7 93.9 reduce-scatter.34
where the time goes:
time: 2080 us; the launch traced here: 2070 us
  waiting for transfers between devices  1220 us (59%)
  blocking collectives  331 us (16%)
  matrix products  220 us (11%)
  other arithmetic  154 us (7%)
  local copies, waits for them, and re-layouts  126 us (6%)
    reduce_scatter x4, waiting for transfers between devices, reduce_tokens(): lax.psum_scatter(builder(jnp.int32(0), local_rows * lax.axis_size('col'))...  344 us
    reduce_scatter x8, waiting for transfers between devices, share_features(): return lax.psum_scatter(parts, 'row', scatter_dimension=1, tiled=True)  336 us
    all_gather x4, waiting for transfers between devices, gather_tokens(): return lax.all_gather(tensor, 'col', axis=0, tiled=True)  205 us
    all_gather x8, waiting for transfers between devices, gather_features(): lax.all_gather(for_sending(parts), 'row', axis=1, tiled=True)  185 us
    psum x1, waiting for transfers between devices, body(): lax.psum(grad_query.astype(jnp.bfloat16), 'dp').astype(jnp.float32)  147 us
    psum x1, blocking collectives, body(): lax.psum((product(tokens_one, w_value), product(tokens_one, rank_down)),...  113 us
    dynamic_slice x80, local copies, waits for them, and re-layouts, gla_sequence(): _, earlier = lax.scan(advance, initial, (updates, fading))  91.4 us
    psum x1, blocking collectives, body(): value_grad = lax.psum(value_part, 'row').astype(jnp.bfloat16)  78.9 us
  transfers between devices with their start and end apart: 25, of which 21 were waited for; matrix products, arithmetic and copies ran while one was open for 17% of the time, Pallas kernels for 0%

commit v1 on v0

--- a/solution.py
+++ b/solution.py
@@ -11,6 +11,27 @@
 SLOT = 1280
 EPSILON = 1e-06
 HIGHEST = lax.Precision.HIGHEST
+
+
+def gather_around(shard, axis, dim):
+    size, index, rows = (lax.axis_size(axis), lax.axis_index(axis), shard.shape[dim])
+    right = [(i, (i + 1) % size) for i in range(size)]
+    left = [(i, (i - 1) % size) for i in range(size)]
+    whole = jnp.zeros((*shard.shape[:dim], size * rows, *shard.shape[dim + 1 :]), shard.dtype)
+    whole = lax.dynamic_update_slice_in_dim(whole, shard, index * rows, axis=dim)
+    from_left = from_right = shard
+    halfway = size // 2
+    for step in range(1, halfway + 1):
+        from_left = lax.ppermute(from_left, axis, right)
+        whole = lax.dynamic_update_slice_in_dim(
+            whole, from_left, (index - step) % size * rows, axis=dim
+        )
+        if step < size - halfway:
+            from_right = lax.ppermute(from_right, axis, left)
+            whole = lax.dynamic_update_slice_in_dim(
+                whole, from_right, (index + step) % size * rows, axis=dim
+            )
+    return whole
 
 
 def for_sending(x):
@@ -88,7 +109,7 @@
 
 
 def gather_tokens(tensor):
-    return lax.all_gather(tensor, "col", axis=0, tiled=True)
+    return gather_around(tensor, "col", 0)
 
 
 def share_features(parts):

time: 2080 us -> 2000 us (0.962)
  waiting for transfers between devices: 1220 us -> 1080 us
  starting transfers between devices: 2.54 us -> 58.5 us
    all_gather x4 -> x0, waiting for transfers between devices: 205 us -> none  [gather_tokens(): return lax.all_gather(tensor, 'col', axis=0, tiled=True)]
    ppermute x0 -> x12, waiting for transfers between devices: none -> 163 us  [the longest x8 135 us: gather_around(): from_left = lax.ppermute(from_left, axis, right)]
    ppermute x0 -> x12, starting transfers between devices: none -> 56.1 us  [the longest x8 46.8 us: gather_around(): from_left = lax.ppermute(from_left, axis, right)]
    reduce_scatter x8, waiting for transfers between devices: 336 us -> 282 us  [share_features(): return lax.psum_scatter(parts, 'row', scatter_dimension=1, tiled=True)]
    reduce_scatter x4, waiting for transfers between devices: 344 us -> 299 us  [reduce_tokens(): lax.psum_scatter(builder(jnp.int32(0), local_rows * lax.axis_size('col'))...]
  transfers between devices with their start and end apart: 25 -> 33, of which waited for: 21 -> 29; matrix products, arithmetic and copies ran while one was open for 17% -> 18% of each run, Pallas kernels for 0% -> 0%
where the time goes in v1:
time: 2000 us; the launch traced here: 1990 us
  waiting for transfers between devices  1080 us (54%)
  blocking collectives  328 us (16%)
  matrix products  217 us (11%)
  other arithmetic  149 us (7%)
  local copies, waits for them, and re-layouts  140 us (7%)
  starting transfers between devices  58.5 us (3%)
    reduce_scatter x4, waiting for transfers between devices, reduce_tokens(): lax.psum_scatter(builder(jnp.int32(0), local_rows * lax.axis_size('col'))...  299 us
    reduce_scatter x8, waiting for transfers between devices, share_features(): return lax.psum_scatter(parts, 'row', scatter_dimension=1, tiled=True)  282 us
    all_gather x8, waiting for transfers between devices, gather_features(): lax.all_gather(for_sending(parts), 'row', axis=1, tiled=True)  183 us
    psum x1, waiting for transfers between devices, body(): lax.psum(grad_query.astype(jnp.bfloat16), 'dp').astype(jnp.float32)  148 us
    ppermute x8, waiting for transfers between devices, gather_around(): from_left = lax.ppermute(from_left, axis, right)  135 us
    psum x1, blocking collectives, body(): lax.psum((product(tokens_one, w_value), product(tokens_one, rank_down)),...  110 us
    dynamic_slice x80, local copies, waits for them, and re-layouts, gla_sequence(): _, earlier = lax.scan(advance, initial, (updates, fading))  91.2 us
    psum x1, blocking collectives, body(): value_grad = lax.psum(value_part, 'row').astype(jnp.bfloat16)  78.4 us
  transfers between devices with their start and end apart: 33, of which 29 were waited for; matrix products, arithmetic and copies ran while one was open for 18% of the time, Pallas kernels for 0%

profile of v1, /device:TPU:0, one launch (start us, length us, event | category | flops | bytes accessed | tf_op | source)
XLA Modules:
  0.0 1985.0 jit_solution(16263508365924455028)
XLA Ops:
  8.7 5.8 psum.168
  22.3 15.8 collective-permute-done
  38.1 9.4 collective-permute-start.2
  52.9 11.2 collective-permute-done.2
  70.9 5.0 fusion.79
  76.7 5.2 fusion.80
  84.5 110.2 %all-reduce.10 = (bf16[1280,16]{0,1:T(8,128)(2,1)}, bf16[1280,512]{1,0:T(8,128)(2,1)}) all-reduce(f32[1280,16]{0,1:T(8,128)S(1)} %fusion.78, f32[1280,512]{1,0:T(8,128)} %fusion.80), channel_id=1, replica_groups=mesh['dp'=4,'row'=2,'col'=4] {'row'}, use_global_device_ids=true, to_apply=%region_3.4 | all-reduce | flops 675840 | bytes 4055040 | tf_op jit(solution)/shard_map/psum | solution.py:176
  206.1 7.1 convolution_bitcast_fusion.1
  213.2 5.3 broadcast.114.clone
  218.5 51.7 %while.34 = (s32[]{:T(128)}, f32[1,256,512]{2,1,0:T(8,128)S(1)}, f32[20,1,256,512]{3,2,1,0:T(8,128)}, f32[20,1,256,1]{2,3,1,0:T(1,128)}, f32[20,1,256]{2,1,0:T(1...) while((s32[]{:T(128)}, f32[1,256,512]{2,1,0:T(8,128)S(1)}, ...), condition=%wide.region_8.9_spmd.clone, body=%wide.region_7.8_spmd.clone.sunk | while | flops 524291 | bytes 2627688 | solution.py:85
  275.5 12.0 fusion.10
  288.0 5.0 fusion.82
  293.7 32.7 %reduce-scatter.17.cloned.1.call-done = f32[1280,256]{1,0:T(8,128)} async-done(((f32[1280,512]{1,0:T(8,128)}), f32[1280,256]{1,0:T(8,128)}) %reduce-scatter.17.cloned.1.call-update) | async-done | bytes 1310736 | tf_op jit(solution)/shard_map/reduce_scatter | solution.py:116
  328.0 5.0 psum.171
  333.0 33.8 %reduce-scatter.19.cloned.1.call-done = f32[1280,256]{1,0:T(8,128)} async-done(((f32[1280,512]{1,0:T(8,128)}), f32[1280,256]{1,0:T(8,128)}) %reduce-scatter.19.cloned.1.call-update) | async-done | bytes 1310736 | tf_op jit(solution)/shard_map/reduce_scatter | solution.py:116
  369.8 24.3 %all-gather.9.cloned.1.call-done = bf16[1280,512]{1,0:T(8,128)(2,1)} async-done(((bf16[1280,256]{1,0:T(8,128)(2,1)}), bf16[1280,512]{1,0:T(8,128)(2,1)}) %all-gather.9.cloned.1.call-update) | async-done | bytes 1310736 | tf_op jit(solution)/shard_map/all_gather | solution.py:122
  394.1 5.5 fusion.83
  405.6 27.1 %collective-permute-done.6 = bf16[320,1024]{1,0:T(8,128)(2,1)S(1)} collective-permute-done((bf16[320,1024]{1,0:T(8,128)(2,1)S(1)}, bf16[320,1024]{1,0:T(8,128)(2,1)S(1)}, u32[]{:S(2)}, u32[]{:S(2)}) %collective-permute-start.6) | collective-permute-done | bytes 655392 | tf_op jit(solution)/shard_map/ppermute | solution.py:25
  432.8 20.6 %collective-permute-start.8 = (bf16[320,1024]{1,0:T(8,128)(2,1)S(1)}, bf16[320,1024]{1,0:T(8,128)(2,1)S(1)}, u32[]{:S(2)}, u32[]{:S(2)}) collective-permute-start(bf16[320,1024]{1,0:T(8,128)(2,1)S(1)} %collective-permute-done.6), channel_id=1, source_target_pairs={{0,1},{1,2},{2,3},{3,0},{4,5},{5,6},{6,7},{7,4},{8,9},{9,10},{10,1... | collective-permute-start | bytes 1966088 | tf_op jit(solution)/shard_map/ppermute | solution.py:25
  453.4 11.2 collective-permute-done.7
  464.7 23.1 %collective-permute-done.8 = bf16[320,1024]{1,0:T(8,128)(2,1)S(1)} collective-permute-done((bf16[320,1024]{1,0:T(8,128)(2,1)S(1)}, bf16[320,1024]{1,0:T(8,128)(2,1)S(1)}, u32[]{:S(2)}, u32[]{:S(2)}) %collective-permute-start.8) | collective-permute-done | bytes 655392 | tf_op jit(solution)/shard_map/ppermute | solution.py:25
  489.4 6.0 fusion.87
  496.8 36.6 %reduce-scatter.21.cloned.1.call-done = f32[320,1024]{1,0:T(8,128)} async-done(((f32[1280,1024]{1,0:T(8,128)}), f32[320,1024]{1,0:T(8,128)}) %reduce-scatter.21.cloned.1.call-update) | async-done | bytes 1310736 | tf_op jit(solution)/shard_map/reduce_scatter | solution.py:128
  536.5 5.0 psum.172
  547.1 15.6 collective-permute-done.3
  562.8 11.9 collective-permute-done.4
  574.8 14.2 collective-permute-done.5
  590.6 6.4 fusion.84
  597.0 9.5 fusion.85
  606.6 15.1 reduce-scatter.29.cloned.1.call-done
  621.7 89.5 %reduce-scatter.23.cloned.1.call-done = f32[1280,704]{0,1:T(8,128)} async-done(((f32[1280,1408]{0,1:T(8,128)}), f32[1280,704]{0,1:T(8,128)}) %reduce-scatter.23.cloned.1.call-update) | async-done | bytes 3604496 | tf_op jit(solution)/shard_map/reduce_scatter | solution.py:116
  711.2 89.4 %reduce-scatter.25.cloned.1.call-done = f32[1280,704]{0,1:T(8,128)} async-done(((f32[1280,1408]{0,1:T(8,128)}), f32[1280,704]{0,1:T(8,128)}) %reduce-scatter.25.cloned.1.call-update) | async-done | bytes 3604496 | tf_op jit(solution)/shard_map/reduce_scatter | solution.py:116
  800.5 6.6 multiply_convert_fusion
  808.7 48.7 %all-gather.13.cloned.1.call-done = bf16[1280,1408]{0,1:T(8,128)(2,1)} async-done(((bf16[1280,704]{0,1:T(8,128)(2,1)}), bf16[1280,1408]{0,1:T(8,128)(2,1)}) %all-gather.13.cloned.1.call-update) | async-done | bytes 3604496 | tf_op jit(solution)/shard_map/all_gather | solution.py:122
  857.5 8.0 fusion.88
  865.5 44.3 %all-gather.15.cloned.1.call-done = bf16[1280,1408]{0,1:T(8,128)(2,1)} async-done(((bf16[1280,704]{0,1:T(8,128)(2,1)}), bf16[1280,1408]{0,1:T(8,128)(2,1)}) %all-gather.15.cloned.1.call-update) | async-done | bytes 3604496 | tf_op jit(solution)/shard_map/all_gather | solution.py:122
  909.8 11.2 convolution_add_fusion
  921.0 40.9 %all-gather.11.cloned.1.call-done = bf16[1280,1408]{0,1:T(8,128)(2,1)} async-done(((bf16[1280,704]{0,1:T(8,128)(2,1)}), bf16[1280,1408]{0,1:T(8,128)(2,1)}) %all-gather.11.cloned.1.call-update) | async-done | bytes 3604496 | tf_op jit(solution)/shard_map/all_gather | solution.py:122
  962.0 8.0 fusion.86
  970.1 88.7 %reduce-scatter.31.cloned.1.call-done = f32[320,1024]{1,0:T(8,128)} async-done(((f32[1280,1024]{1,0:T(8,128)}), f32[320,1024]{1,0:T(8,128)}) %reduce-scatter.31.cloned.1.call-update) | async-done | bytes 1310736 | tf_op jit(solution)/shard_map/reduce_scatter | solution.py:128
  1058.8 97.1 %reduce-scatter.27.cloned.1.call-done = f32[320,1024]{1,0:T(8,128)} async-done(((f32[1280,1024]{1,0:T(8,128)}), f32[320,1024]{1,0:T(8,128)}) %reduce-scatter.27.cloned.1.call-update) | async-done | bytes 1310736 | tf_op jit(solution)/shard_map/reduce_scatter | solution.py:128
  1171.2 15.7 collective-permute-done.9
  1186.9 10.4 collective-permute-start.11
  1200.3 12.4 collective-permute-done.11
  1219.1 7.8 convolution_convert_fusion.1
  1226.9 5.7 convolution_convert_fusion.2
  1232.6 21.2 %reduce-scatter.33.cloned.1.call-done = f32[1280,256]{1,0:T(8,128)} async-done(((f32[1280,512]{1,0:T(8,128)}), f32[1280,256]{1,0:T(8,128)}) %reduce-scatter.33.cloned.1.call-update) | async-done | bytes 1310736 | tf_op jit(solution)/shard_map/reduce_scatter | solution.py:116
  1257.5 5.0 psum.174
  1265.2 8.5 convolution_convert_fusion
  1276.7 12.8 all-gather.17.cloned.1.call-done
  1289.5 9.7 convolution_bitcast_fusion
  1299.2 10.7 fusion.5
  1312.7 5.3 broadcast.114
  1318.0 136.4 %while.35 = (s32[]{:T(128)}, f32[1,256,512]{2,1,0:T(8,128)S(1)}, f32[20,1,256,512]{3,2,1,0:T(8,128)}, f32[20,1,256]{2,1,0:T(1,128)S(1)}, f32[20,1,256,512]{2,3,0...) while((s32[]{:T(128)}, f32[1,256,512]{2,1,0:T(8,128)S(1)}, ...), condition=%wide.region_28.29_spmd.clone, body=%wide.region_26.28_spmd.clone.sunk | while | flops 786180 | bytes 5249168 | solution.py:85
  1454.5 10.9 fusion.50
  1465.5 9.8 fusion.13
  1482.9 78.4 %all-reduce.11 = bf16[1280,512]{1,0:T(8,128)(2,1)S(1)} all-reduce(f32[1280,512]{1,0:T(8,128)} %bitcast.223), channel_id=1, replica_groups=mesh['dp'=4,'row'=2,'col'=4] {'row'}, use_global_device_ids=true, to_apply=%region_29.30 | all-reduce | flops 655360 | bytes 3932160 | tf_op jit(solution)/shard_map/psum | solution.py:265
  1574.9 11.5 all-gather.19.cloned.1.call-done
  1608.7 23.4 %all-reduce.3 = (bf16[16,512]{1,0:T(8,128)(2,1)S(1)}, bf16[512]{0:T(512)(128)(2,1)S(1)}) all-reduce(bf16[16,512]{1,0:T(8,128)(2,1)S(1)} %convolution_dynamic-update-slice_fusion, bf16[512]{0:T(512)(128)(2,1)S(1)} %dynamic_update_slice.98), channel_id=1, replica_groups=mesh['dp'=4,'row'=2,'col'=4] {'dp','row'}, use_global_device_ids=true, to_apply=%region_43.44 | all-reduce | flops 8704 | bytes 34816 | tf_op jit(solution)/shard_map/psum | solution.py:327
  1634.0 38.8 %psum.176 = bf16[1280,16]{0,1:T(8,128)(2,1)S(1)} all-reduce(f32[1280,16]{0,1:T(8,128)S(1)} %fusion.60), channel_id=1, replica_groups=mesh['dp'=4,'row'=2,'col'=4] {'row','col'}, use_global_device_ids=true, to_apply=%region_33.34 | all-reduce | flops 20480 | bytes 122880 | tf_op jit(solution)/shard_map/psum | solution.py:292
  1675.0 12.6 psum.183
  1688.3 148.1 %all-reduce.9.cloned.1.call-done = (bf16[1024,512]{1,0:T(8,128)(2,1)}, bf16[1024,512]{1,0:T(8,128)(2,1)}, bf16[1024,512]{1,0:T(8,128)(2,1)}, bf16[1024,512]{1,0:...) async-done(((bf16[1024,512]{1,0:T(8,128)(2,1)}, bf16[1024,512]{1,0:T(8,128)(2,1)}, ...) | async-done | bytes 13893648 | tf_op jit(solution)/shard_map/psum | solution.py:315
  1855.7 76.9 %reduce-scatter.35.cloned.1.call-done = f32[320,1024]{1,0:T(8,128)} async-done(((f32[1280,1024]{1,0:T(8,128)}), f32[320,1024]{1,0:T(8,128)}) %reduce-scatter.35.cloned.1.call-update) | async-done | bytes 1310736 | tf_op jit(solution)/shard_map/reduce_scatter | solution.py:128
  1940.6 33.8 %all-reduce.1 = (f32[1024]{0:T(1024)}, f32[256]{0:T(256)}, f32[1024]{0:T(1024)}) all-reduce(f32[1024]{0:T(1024)S(1)} %get-tuple-element.257, f32[256]{0:T(256)S(1)} %copy-done.73, f32[1024]{0:T(1024)S(1)} %copy-done.68), channel_id=1, replica_groups=mesh['dp'=4,'row'=2,'col'=4] {'dp','col'}, use_global_device_ids=true, to_apply=%region_37.38 | all-reduce | flops 2304 | bytes 18432 | tf_op jit(solution)/shard_map/psum | solution.py:325
  (522 shorter events, 369.9 us)
Async XLA Ops:
  7.2 583.4 %copy-start = (bf16[1024,1408]{1,0:T(8,128)(2,1)S(1)}, bf16[1024,1408]{1,0:T(8,128)(2,1)}, u32[]{:S(2)}) copy-start(bf16[1024,1408]{1,0:T(8,128)(2,1)} %param.34) | copy-start | bytes 8650756
  7.2 192.2 %reduce-scatter.13.cloned.1.call-start = ((), (), s32[]{:S(2)}) async-start(), calls=%async_computation.12 | async-start | bytes 3932160 | tf_op jit(solution)/shard_map/reduce_scatter | solution.py:116
  18.2 19.9 %collective-permute-start = (bf16[320,1024]{1,0:T(8,128)(2,1)S(1)}, bf16[320,1024]{1,0:T(8,128)(2,1)}, u32[]{:S(2)}, u32[]{:S(2)}) collective-permute-start(bf16[320,1024]{1,0:T(8,128)(2,1)S(1)} %get-tuple-element.314), channel_id=1, source_target_pairs={{0,1},{1,2},{2,3},{3,0},{4,5},{5,6},{6,7},{7,4},{8,9},{9,10},{10,1... | collective-permute-start | bytes 1966088 | tf_op jit(solution)/shard_map/ppermute | solution.py:25
  20.3 30.7 %collective-permute-start.1 = (bf16[320,1024]{1,0:T(8,128)(2,1)S(1)}, bf16[320,1024]{1,0:T(8,128)(2,1)}, u32[]{:S(2)}, u32[]{:S(2)}) collective-permute-start(bf16[320,1024]{1,0:T(8,128)(2,1)S(1)} %get-tuple-element.314), channel_id=1, source_target_pairs={{0,3},{1,0},{2,1},{3,2},{4,7},{5,4},{6,5},{7,6},{8,11},{9,8},{10,9... | collective-permute-start | bytes 1966088 | tf_op jit(solution)/shard_map/ppermute | solution.py:30
  38.1 26.0 %collective-permute-start.2 = (bf16[320,1024]{1,0:T(8,128)(2,1)}, bf16[320,1024]{1,0:T(8,128)(2,1)}, u32[]{:S(2)}, u32[]{:S(2)}) collective-permute-start(bf16[320,1024]{1,0:T(8,128)(2,1)} %collective-permute-done), channel_id=1, source_target_pairs={{0,1},{1,2},{2,3},{3,0},{4,5},{5,6},{6,7},{7,4},{8,9},{9,10},{10,1... | collective-permute-start | bytes 1966088 | tf_op jit(solution)/shard_map/ppermute | solution.py:25
  49.5 16.6 copy-start.82
  70.9 133.1 %reduce-scatter.15.cloned.1.call-start = ((), (), s32[]{:S(2)}) async-start(), calls=%async_computation.13 | async-start | bytes 3932160 | tf_op jit(solution)/shard_map/reduce_scatter | solution.py:116
  76.0 250.4 %reduce-scatter.17.cloned.1.call-start = ((), (), s32[]{:S(2)}) async-start(), calls=%async_computation.14 | async-start | bytes 3932160 | tf_op jit(solution)/shard_map/reduce_scatter | solution.py:116
  76.7 193.5 %copy-start.53 = (f32[64,64]{1,0:T(8,128)}, f32[64,64]{1,0:T(8,128)S(1)}, u32[]{:S(2)}) copy-start(f32[64,64]{1,0:T(8,128)S(1)} %fusion.52) | copy-start | bytes 49156
  84.5 110.2 %copy-start.71 = (bf16[16,512]{1,0:T(8,128)(2,1)S(1)}, bf16[16,512]{1,0:T(8,128)(2,1)}, u32[]{:S(2)}) copy-start(bf16[16,512]{1,0:T(8,128)(2,1)} %param.29) | copy-start | bytes 49156
  287.5 79.3 %reduce-scatter.19.cloned.1.call-start = ((), (), s32[]{:S(2)}) async-start(), calls=%async_computation.15 | async-start | bytes 3932160 | tf_op jit(solution)/shard_map/reduce_scatter | solution.py:116
  293.0 101.1 %all-gather.9.cloned.1.call-start = ((), (), s32[]{:S(2)}) async-start(), calls=%async_computation.16 | async-start | bytes 1966080 | tf_op jit(solution)/shard_map/all_gather | solution.py:122
  293.7 76.1 %copy-start.69 = (f32[256]{0:T(256)}, f32[256]{0:T(256)S(1)}, u32[]{:S(2)}) copy-start(f32[256]{0:T(256)S(1)} %convert_element_type.167) | copy-start | bytes 3076
  369.8 163.6 %reduce-scatter.21.cloned.1.call-start = ((), (), s32[]{:S(2)}) async-start(), calls=%async_computation.17 | async-start | bytes 6553600 | tf_op jit(solution)/shard_map/reduce_scatter | solution.py:128
  399.7 222.0 %reduce-scatter.29.cloned.1.call-start = ((), (), s32[]{:S(2)}) async-start(), calls=%async_computation.22 | async-start | bytes 10813440 | tf_op jit(solution)/shard_map/reduce_scatter | solution.py:116
  401.8 31.0 %collective-permute-start.6 = (bf16[320,1024]{1,0:T(8,128)(2,1)S(1)}, bf16[320,1024]{1,0:T(8,128)(2,1)S(1)}, u32[]{:S(2)}, u32[]{:S(2)}) collective-permute-start(bf16[320,1024]{1,0:T(8,128)(2,1)S(1)} %get-tuple-element.306), channel_id=1, source_target_pairs={{0,1},{1,2},{2,3},{3,0},{4,5},{5,6},{6,7},{7,4},{8,9},{9,10},{10,1... | collective-permute-start | bytes 1966088 | tf_op jit(solution)/shard_map/ppermute | solution.py:25
  403.3 61.4 %collective-permute-start.7 = (bf16[320,1024]{1,0:T(8,128)(2,1)S(1)}, bf16[320,1024]{1,0:T(8,128)(2,1)S(1)}, u32[]{:S(2)}, u32[]{:S(2)}) collective-permute-start(bf16[320,1024]{1,0:T(8,128)(2,1)S(1)} %get-tuple-element.306), channel_id=1, source_target_pairs={{0,3},{1,0},{2,1},{3,2},{4,7},{5,4},{6,5},{7,6},{8,11},{9,8},{10,9... | collective-permute-start | bytes 1966088 | tf_op jit(solution)/shard_map/ppermute | solution.py:30
  432.8 55.0 %collective-permute-start.8 = (bf16[320,1024]{1,0:T(8,128)(2,1)S(1)}, bf16[320,1024]{1,0:T(8,128)(2,1)S(1)}, u32[]{:S(2)}, u32[]{:S(2)}) collective-permute-start(bf16[320,1024]{1,0:T(8,128)(2,1)S(1)} %collective-permute-done.6), channel_id=1, source_target_pairs={{0,1},{1,2},{2,3},{3,0},{4,5},{5,6},{6,7},{7,4},{8,9},{9,10},{10,1... | collective-permute-start | bytes 1966088 | tf_op jit(solution)/shard_map/ppermute | solution.py:25
  453.4 36.0 %copy-start.76 = (bf16[1408,1024]{1,0:T(8,128)(2,1)S(1)}, bf16[1408,1024]{1,0:T(8,128)(2,1)}, u32[]{:S(2)}) copy-start(bf16[1408,1024]{1,0:T(8,128)(2,1)} %param.36) | copy-start | bytes 8650756
  495.4 38.0 %copy-start.20 = (bf16[320,1024]{1,0:T(8,128)(2,1)S(1)}, bf16[320,1024]{1,0:T(8,128)(2,1)}, u32[]{:S(2)}) copy-start(bf16[320,1024]{1,0:T(8,128)(2,1)} %param.21) | copy-start | bytes 1966084
  495.4 215.8 %reduce-scatter.23.cloned.1.call-start = ((), (), s32[]{:S(2)}) async-start(), calls=%async_computation.18 | async-start | bytes 10813440 | tf_op jit(solution)/shard_map/reduce_scatter | solution.py:116
  543.3 19.5 collective-permute-start.3
  544.5 30.2 %collective-permute-start.4 = (bf16[320,1024]{1,0:T(8,128)(2,1)S(1)}, bf16[320,1024]{1,0:T(8,128)(2,1)S(1)}, u32[]{:S(2)}, u32[]{:S(2)}) collective-permute-start(bf16[320,1024]{1,0:T(8,128)(2,1)S(1)} %get-tuple-element.308), channel_id=1, source_target_pairs={{0,3},{1,0},{2,1},{3,2},{4,7},{5,4},{6,5},{7,6},{8,11},{9,8},{10,9... | collective-permute-start | bytes 1966088 | tf_op jit(solution)/shard_map/ppermute | solution.py:30
  562.8 26.3 %collective-permute-start.5 = (bf16[320,1024]{1,0:T(8,128)(2,1)S(1)}, bf16[320,1024]{1,0:T(8,128)(2,1)S(1)}, u32[]{:S(2)}, u32[]{:S(2)}) collective-permute-start(bf16[320,1024]{1,0:T(8,128)(2,1)S(1)} %collective-permute-done.3), channel_id=1, source_target_pairs={{0,1},{1,2},{2,3},{3,0},{4,5},{5,6},{6,7},{7,4},{8,9},{9,10},{10,1... | collective-permute-start | bytes 1966088 | tf_op jit(solution)/shard_map/ppermute | solution.py:25
  597.0 203.5 %reduce-scatter.25.cloned.1.call-start = ((), (), s32[]{:S(2)}) async-start(), calls=%async_computation.19 | async-start | bytes 10813440 | tf_op jit(solution)/shard_map/reduce_scatter | solution.py:116
  606.5 250.9 %all-gather.13.cloned.1.call-start = ((), (), s32[]{:S(2)}) async-start(), calls=%async_computation.23 | async-start | bytes 5406720 | tf_op jit(solution)/shard_map/all_gather | solution.py:122
  807.2 102.6 %all-gather.15.cloned.1.call-start = ((), (), s32[]{:S(2)}) async-start(), calls=%async_computation.24 | async-start | bytes 5406720 | tf_op jit(solution)/shard_map/all_gather | solution.py:122
  807.9 154.1 %all-gather.11.cloned.1.call-start = ((), (), s32[]{:S(2)}) async-start(), calls=%async_computation.20 | async-start | bytes 5406720 | tf_op jit(solution)/shard_map/all_gather | solution.py:122
  808.5 250.3 %reduce-scatter.31.cloned.1.call-start = ((), (), s32[]{:S(2)}) async-start(), calls=%async_computation.25 | async-start | bytes 6553600 | tf_op jit(solution)/shard_map/reduce_scatter | solution.py:128
  921.0 41.0 %copy-start.77 = (bf16[1408,1024]{1,0:T(8,128)(2,1)S(1)}, bf16[1408,1024]{1,0:T(8,128)(2,1)}, u32[]{:S(2)}) copy-start(bf16[1408,1024]{1,0:T(8,128)(2,1)} %param.36) | copy-start | bytes 8650756
  921.0 234.9 %reduce-scatter.27.cloned.1.call-start = ((), (), s32[]{:S(2)}) async-start(), calls=%async_computation.21 | async-start | bytes 6553600 | tf_op jit(solution)/shard_map/reduce_scatter | solution.py:128
  970.0 185.9 %copy-start.18 = (f32[320,1024]{1,0:T(8,128)S(1)}, f32[320,1024]{1,0:T(8,128)}, u32[]{:S(2)}) copy-start(f32[320,1024]{1,0:T(8,128)} %get-tuple-element.310) | copy-start | bytes 3932164
  970.0 185.9 %copy-start.63 = (f32[320]{0:T(512)S(1)}, f32[320]{0:T(512)}, u32[]{:S(2)}) copy-start(f32[320]{0:T(512)} %copy-done.62) | copy-start | bytes 3844
  970.0 283.8 %reduce-scatter.33.cloned.1.call-start = ((), (), s32[]{:S(2)}) async-start(), calls=%async_computation.26 | async-start | bytes 3932160 | tf_op jit(solution)/shard_map/reduce_scatter | solution.py:116
  1167.4 19.5 collective-permute-start.9
  1168.9 31.3 %collective-permute-start.10 = (bf16[320,1024]{1,0:T(8,128)(2,1)S(1)}, bf16[320,1024]{1,0:T(8,128)(2,1)S(1)}, u32[]{:S(2)}, u32[]{:S(2)}) collective-permute-start(bf16[320,1024]{1,0:T(8,128)(2,1)S(1)} %get-tuple-element.303), channel_id=1, source_target_pairs={{0,3},{1,0},{2,1},{3,2},{4,7},{5,4},{6,5},{7,6},{8,11},{9,8},{10,9... | collective-permute-start | bytes 1966088 | tf_op jit(solution)/shard_map/ppermute | solution.py:30
  1186.9 25.8 %collective-permute-start.11 = (bf16[320,1024]{1,0:T(8,128)(2,1)S(1)}, bf16[320,1024]{1,0:T(8,128)(2,1)S(1)}, u32[]{:S(2)}, u32[]{:S(2)}) collective-permute-start(bf16[320,1024]{1,0:T(8,128)(2,1)S(1)} %collective-permute-done.9), channel_id=1, source_target_pairs={{0,1},{1,2},{2,3},{3,0},{4,5},{5,6},{6,7},{7,4},{8,9},{9,10},{10,1... | collective-permute-start | bytes 1966088 | tf_op jit(solution)/shard_map/ppermute | solution.py:25
  1197.3 16.9 copy-start.80
  1217.4 72.1 %all-gather.17.cloned.1.call-start = ((), (), s32[]{:S(2)}) async-start(), calls=%async_computation.27 | async-start | bytes 1966080 | tf_op jit(solution)/shard_map/all_gather | solution.py:122
  1226.9 26.9 %copy-start.16 = (f32[1280,256]{1,0:T(8,128)S(1)}, f32[1280,256]{1,0:T(8,128)}, u32[]{:S(2)}) copy-start(f32[1280,256]{1,0:T(8,128)} %reduce-scatter.17.cloned.1.call-done) | copy-start | bytes 3932164
  1226.9 26.9 %copy-start.24 = (f32[1280,256]{1,0:T(8,128)S(1)}, f32[1280,256]{1,0:T(8,128)}, u32[]{:S(2)}) copy-start(f32[1280,256]{1,0:T(8,128)} %reduce-scatter.19.cloned.1.call-done) | copy-start | bytes 3932164
  1226.9 26.9 %copy-start.70 = (f32[256]{0:T(256)S(1)}, f32[256]{0:T(256)}, u32[]{:S(2)}) copy-start(f32[256]{0:T(256)} %copy-done.69) | copy-start | bytes 3076
  1265.1 300.5 %all-gather.23.cloned.1.call-start = ((), (), s32[]{:S(2)}) async-start(), calls=%async_computation.30 | async-start | bytes 1966080 | tf_op jit(solution)/shard_map/all_gather | solution.py:122
  1273.6 15.8 copy-start.9
  1276.2 294.0 %all-gather.21.cloned.1.call-start = ((), (), s32[]{:S(2)}) async-start(), calls=%async_computation.29 | async-start | bytes 1966080 | tf_op jit(solution)/shard_map/all_gather | solution.py:122
  1299.2 10.7 copy-start.29
  1318.0 136.5 %copy-start.4 = (f32[1280,256]{1,0:T(8,128)S(1)}, f32[1280,256]{1,0:T(8,128)}, u32[]{:S(2)}) copy-start(f32[1280,256]{1,0:T(8,128)} %copy-done.3) | copy-start | bytes 3932164
  1318.0 136.5 %copy-start.7 = (f32[1,20,64,256]{3,2,1,0:T(8,128)S(1)}, f32[1,20,64,256]{3,2,1,0:T(8,128)}, u32[]{:S(2)}) copy-start(f32[1,20,64,256]{3,2,1,0:T(8,128)} %copy-done.5) | copy-start | bytes 3932164
  1318.0 136.5 %copy-start.52 = (f32[1,20,1,256]{3,1,2,0:T(8,128)S(1)}, f32[1,20,1,256]{3,1,2,0:T(8,128)}, u32[]{:S(2)}) copy-start(f32[1,20,1,256]{3,1,2,0:T(8,128)} %copy-done.51) | copy-start | bytes 61444
  1454.5 11.0 copy-start.2
  1465.5 9.9 copy-start.13
  1465.5 9.9 copy-start.15
  1465.5 9.9 copy-start.54
  1482.8 103.6 %all-gather.19.cloned.1.call-start = ((), (), s32[]{:S(2)}) async-start(), calls=%async_computation.28 | async-start | bytes 1966080 | tf_op jit(solution)/shard_map/all_gather | solution.py:122
  1561.3 275.1 %all-reduce.9.cloned.1.call-start = ((), (), s32[]{:S(2)}) async-start(), calls=%async_computation.32 | async-start | bytes 27787264 | tf_op jit(solution)/shard_map/psum | solution.py:315
  1591.1 341.6 %reduce-scatter.35.cloned.1.call-start = ((), (), s32[]{:S(2)}) async-start(), calls=%async_computation.31 | async-start | bytes 6553600 | tf_op jit(solution)/shard_map/reduce_scatter | solution.py:128
  1607.8 25.5 %copy-start.72 = (bf16[16,512]{1,0:T(8,128)(2,1)S(1)}, bf16[16,512]{1,0:T(8,128)(2,1)}, u32[]{:S(2)}) copy-start(bf16[16,512]{1,0:T(8,128)(2,1)} %param.29) | copy-start | bytes 49156
  1854.1 78.5 %copy-start.21 = (bf16[320,1024]{1,0:T(8,128)(2,1)S(1)}, bf16[320,1024]{1,0:T(8,128)(2,1)}, u32[]{:S(2)}) copy-start(bf16[320,1024]{1,0:T(8,128)(2,1)} %param.21) | copy-start | bytes 1966084
  1854.1 78.5 %copy-start.57 = (bf16[1024,16]{0,1:T(8,128)(2,1)S(1)}, bf16[1024,16]{0,1:T(8,128)(2,1)}, u32[]{:S(2)}) copy-start(bf16[1024,16]{0,1:T(8,128)(2,1)} %param.28) | copy-start | bytes 98308
  1854.1 78.5 %copy-start.59 = (f32[1024]{0:T(1024)S(1)}, f32[1024]{0:T(1024)}, u32[]{:S(2)}) copy-start(f32[1024]{0:T(1024)} %copy-done.58) | copy-start | bytes 12292
  1854.1 78.5 %copy-start.65 = (f32[320]{0:T(512)S(1)}, f32[320]{0:T(512)}, u32[]{:S(2)}) copy-start(f32[320]{0:T(512)} %copy-done.64) | copy-start | bytes 3844
  1855.7 84.9 %copy-start.67 = (f32[320]{0:T(512)S(1)}, f32[320]{0:T(512)}, u32[]{:S(2)}) copy-start(f32[320]{0:T(512)} %copy-done.66) | copy-start | bytes 3844
  1855.7 84.9 %copy-start.68 = (f32[1024]{0:T(1024)S(1)}, f32[1024]{0:T(1024)}, u32[]{:S(2)}) copy-start(f32[1024]{0:T(1024)} %get-tuple-element.255) | copy-start | bytes 12292
  1855.7 84.9 %copy-start.73 = (f32[256]{0:T(256)S(1)}, f32[256]{0:T(256)}, u32[]{:S(2)}) copy-start(f32[256]{0:T(256)} %get-tuple-element.253) | copy-start | bytes 3076
  (54 other events, 142.6 us)
Sparse Core Ops, SparseCore 0:
  71.0 55.0 reduce-scatter.12
  129.0 64.9 reduce-scatter.14
  287.6 38.7 reduce-scatter.16
  329.1 37.5 reduce-scatter.18
  369.9 24.2 all-gather.8
  399.8 133.5 reduce-scatter.20
  535.7 85.9 reduce-scatter.28
  624.1 87.0 reduce-scatter.22
  713.5 86.9 reduce-scatter.24
  807.3 50.1 all-gather.12
  859.7 50.0 all-gather.14
  911.8 50.0 all-gather.10
  965.0 93.7 reduce-scatter.30
  1061.6 94.2 reduce-scatter.26
  1217.5 36.2 reduce-scatter.32
  1265.2 24.2 all-gather.16
  1290.9 24.2 all-gather.22
  1482.9 38.3 all-gather.20
  1561.4 24.9 all-gather.18
  1591.2 245.1 all-reduce.8
  1838.7 93.9 reduce-scatter.34
